TPU v7x, 256 devices: a whole 4x4x8 slice. The times are simulated.
256 devices in a mesh: replica: 64 (over x, z, core), shard: 4 (over y).
Axes of the slice: x: 4, y: 4, z: 8, core: 2. Of those that a mesh axis runs over, the one named last changes fastest.
Arguments:
- activations: bfloat16 [65536, 1536], P('replica'), may hold values from -6 to 6
- output_grads: bfloat16 [65536, 4, 1536], P('replica', None, 'shard'), may hold values from -0.00390625 to 0.00390625
- owner: int32 [4], replicated, may hold values from 0 to 3, each once
- step_count: int32 [1], replicated, may hold values from 1 to 40
- statistics: float32 [6144, 2, 1536], P(('replica', 'shard')), may hold values from -6 to 6
- inverse_roots: bfloat16 [6144, 2, 1536], P(('replica', 'shard')), may hold values from -1 to 2, as said below
- first_moment: float32 [6144, 1536], P(('replica', 'shard')), may hold values from -0.6 to 0.6
- second_moment: float32 [6144, 1536], P(('replica', 'shard')), may hold values from 0.005 to 0.05
Outputs:
- new_statistics: float32 [6144, 2, 1536], P(('replica', 'shard'))
- new_first: float32 [6144, 1536], P(('replica', 'shard'))
- new_second: float32 [6144, 1536], P(('replica', 'shard'))
- update: bfloat16 [4, 1536, 1536], P(None, None, 'shard')
Inputs may be any that keep to these rules, and one draw needn't show every extreme that they name: A permutation: block b belongs to the group of replicas b' * (16) to (b' + 1) * 16 - 1 with b' = owner[b]. `inverse_roots`: each matrix has positive diagonal entries.
All inputs are finite; a program needn't handle non-finite values.
Results may differ from a plain program's by a relative error of at most 0.0049.
Values may be sent and summed in bfloat16 or wider, within the bound.
No kernel may reach another device: no remote copies, remote signals or barrier semaphores. Data moves between devices by JAX's collectives and lax.ppermute only.
A program may use at most 128 MiB of HBM per device.

v0:
```python
import functools
import math
import jax
import jax.numpy as jnp
from jax import lax
from jax.sharding import Mesh
from jax.sharding import PartitionSpec as P

REPLICA = ("replica_0", "replica_1", "replica_2")
REPLICA_SHARD = ("replica_0", "replica_1", "replica_2", "shard")
beta_stat = 0.9
beta_first = 0.9
beta_second = 0.999
eps_adam = 1e-08
eps_norm = 1e-06


def in_order(pieces, dim):
    shape = list(pieces.shape[1:])
    shape[dim] *= pieces.shape[0]
    return jnp.moveaxis(pieces, 0, dim).reshape(shape)


def copy_for_each(value, axis):
    copies = jnp.broadcast_to(value, (lax.axis_size(axis), *value.shape))
    return lax.all_to_all(copies, axis, split_axis=0, concat_axis=0, tiled=True)


def gather_directly(value, axis, dim):
    return in_order(copy_for_each(value, axis), dim)


def partner_2(value, axis, apart):
    return lax.ppermute(value, axis, [(i, i ^ 1 << apart) for i in range(lax.axis_size(axis))])


def reduced_to_own(pieces, axes, order):
    shape = [lax.axis_size(a) for a in axes]
    pieces = pieces.reshape(*shape, *pieces.shape[1:])
    pieces = pieces.transpose(*order, *range(len(axes), pieces.ndim))
    pieces = pieces.reshape(-1, *pieces.shape[len(axes) :])
    for k in order:
        pieces = lax.psum_scatter(pieces, axes[k], scatter_dimension=0, tiled=True)
    return pieces[0]


def cut_along(value, dim, length):
    before, after = (value.shape[:dim], value.shape[dim + 1 :])
    return jnp.moveaxis(value.reshape(*before, length, -1, *after), dim, 0)


def scatter_axes(value, axes, order, dim):
    length = lax.axis_size(axes)
    return reduced_to_own(cut_along(value, dim, length), axes, order)


def one_axis_at_a_time(value, axes):
    return functools.reduce(lax.psum, axes, value)


def butterfly(values, concat_axis, group_bits, swap_values):
    position = lax.axis_index(REPLICA)
    for bit_number in range(group_bits):
        partner = swap_values(values, bit_number)
        upper = position >> bit_number & 1 == 1
        values = jnp.where(
            upper,
            jnp.concatenate([partner, values], concat_axis),
            jnp.concatenate([values, partner], concat_axis),
        )
    return values


def body(
    activations,
    output_grads,
    owner,
    step_count,
    statistics,
    inverse_roots,
    first_moment,
    second_moment,
):
    model_width = activations.shape[1]
    blocks_count = output_grads.shape[1]
    replicas = lax.axis_size(REPLICA)
    shards = lax.axis_size("shard")
    group_size = replicas // blocks_count
    group_bits = group_size.bit_length() - 1
    rows_dev = blocks_count * model_width // replicas
    span_rows = statistics.shape[0]
    owner_slot = lax.axis_index(REPLICA) // group_size
    local_index = lax.axis_index(REPLICA) % group_size
    span_index = local_index * shards + lax.axis_index("shard")
    root_rows = gather_directly(inverse_roots[:, 1, :], "shard", 0)
    whole_root = butterfly(
        root_rows, 0, group_bits, lambda values, bit_number: partner_2(values, REPLICA, bit_number)
    )
    slot_ids = jnp.arange(blocks_count, dtype=jnp.int32)
    onehot = (owner[None, :] == slot_ids[:, None]).astype(jnp.int32)
    source = jnp.sum(onehot * slot_ids[None, :], axis=1)
    grads_slot = jnp.take(output_grads, source, axis=1)
    piece_rows = math.gcd(rows_dev * lax.axis_size(REPLICA), model_width)

    def piece_product(piece_number):
        first_row = piece_number * piece_rows
        block_slot = first_row // model_width
        douts = lax.dynamic_index_in_dim(grads_slot, block_slot, 1, keepdims=False)
        return lax.dot_general(
            activations, douts, (((0,), (0,)), ((), ())), preferred_element_type=jnp.float32
        )

    pieces = lax.map(
        piece_product, jnp.arange(rows_dev * lax.axis_size(REPLICA) // piece_rows, dtype=jnp.int32)
    )
    reduced = scatter_axes(
        pieces.reshape(rows_dev * lax.axis_size(REPLICA), pieces.shape[-1]), REPLICA, (2, 0, 1), 0
    )
    exact_rows = lax.all_to_all(
        reduced.astype(jnp.bfloat16), "shard", split_axis=0, concat_axis=1, tiled=True
    ).astype(reduced.dtype)
    rounded = exact_rows.astype(jnp.bfloat16)
    block_rows = gather_directly(rounded, "shard", 0)
    full_grad = butterfly(
        block_rows, 0, group_bits, lambda values, bit_number: partner_2(values, REPLICA, bit_number)
    )
    grad_columns = lax.dynamic_slice_in_dim(full_grad, span_index * span_rows, span_rows, 1)
    left_gram = lax.dot_general(
        rounded, full_grad, (((1,), (1,)), ((), ())), preferred_element_type=jnp.float32
    )
    right_gram = lax.dot_general(
        grad_columns, full_grad, (((0,), (0,)), ((), ())), preferred_element_type=jnp.float32
    )
    new_left = beta_stat * statistics[:, 0, :] + (1.0 - beta_stat) * left_gram
    new_right = beta_stat * statistics[:, 1, :] + (1.0 - beta_stat) * right_gram
    count_float = step_count[0].astype(jnp.float32)
    first_new = beta_first * first_moment + (1.0 - beta_first) * exact_rows
    second_new = beta_second * second_moment + (1.0 - beta_second) * exact_rows * exact_rows
    first_hat = first_new / (1.0 - jnp.power(beta_first, count_float))
    second_hat = second_new / (1.0 - jnp.power(beta_second, count_float))
    adam_dir = first_hat / (jnp.sqrt(second_hat) + eps_adam)
    left_root = inverse_roots[:, 0, :]
    left_part = jnp.dot(left_root, full_grad, preferred_element_type=jnp.float32)
    precond = lax.dot_general(
        left_part,
        whole_root.astype(jnp.float32),
        (((1,), (1,)), ((), ())),
        precision=lax.Precision.HIGHEST,
    )
    slot_mask = (slot_ids == owner_slot).astype(jnp.float32)
    adam_total, precond_total = (
        one_axis_at_a_time(slot_mask * jnp.sum(adam_dir * adam_dir), REPLICA_SHARD),
        one_axis_at_a_time(slot_mask * jnp.sum(precond * precond), REPLICA_SHARD),
    )
    adam_squares = jnp.sum(adam_total * slot_mask)
    precond_squares = jnp.sum(precond_total * slot_mask)
    scale = jnp.sqrt(adam_squares) / (jnp.sqrt(precond_squares) + eps_norm)
    grafted = (precond * scale).astype(jnp.bfloat16)
    feature_rows = lax.all_to_all(grafted, "shard", split_axis=1, concat_axis=0, tiled=True)
    every_block = lax.all_gather(feature_rows, REPLICA, axis=0, tiled=True)
    update = jnp.take(
        every_block.reshape(blocks_count, model_width, every_block.shape[-1]), owner, axis=0
    )
    new_stats = jnp.stack([new_left, new_right], axis=1)
    return (new_stats, first_new, second_new, update)


def solution(mesh):
    torus = Mesh(
        mesh.devices.reshape(4, 8, 2, mesh.shape["shard"]),
        ("replica_0", "replica_1", "replica_2", "shard"),
    )
    placed = (
        P(REPLICA, None),
        P(REPLICA, None, "shard"),
        P(),
        P(),
        P(REPLICA_SHARD, None, None),
        P(REPLICA_SHARD, None, None),
        P(REPLICA_SHARD, None),
        P(REPLICA_SHARD, None),
    )
    return jax.shard_map(
        body,
        mesh=torus,
        in_specs=placed,
        out_specs=(
            P(REPLICA_SHARD, None, None),
            P(REPLICA_SHARD, None),
            P(REPLICA_SHARD, None),
            P(None, None, "shard"),
        ),
        check_vma=False,
    )
```

profile of v0, /device:TPU:1, one launch (start us, length us, event | category | flops | bytes accessed | tf_op | source)
XLA Modules:
  0.0 700.0 jit_solution(6775838303506029115)
XLA Ops:
  9.1 16.4 %gather_fusion = bf16[4,1024,384]{2,0,1:T(4,128)(2,1)} fusion(bf16[1024,4,384]{2,1,0:T(4,128)(2,1)S(1)} %copy-done, s32[1024]{0:T(1024)S(1)} %pad_clamp_fusion.1), kind=kCustom, calls=%fused_computation | custom fusion | bytes 6291472 | tf_op jit(solution)/shard_map/jit(_take)/gather | solution.py:102
  25.5 3.3 select_bitcast_fusion
  30.9 39.4 %while.12 = (s32[]{:T(128)}, f32[4,1536,384]{2,1,0:T(8,128)}, s32[4]{0:T(128)S(1)}, bf16[1024,4,384]{2,0,1:T(8,128)(2,1)}, bf16[1024,1536]{1,0:T(8,128)(2,1)}, /...) while((s32[]{:T(128)}, f32[4,1536,384]{2,1,0:T(8,128)}, ...), condition=%wide.region_2.3_spmd, body=%wide.region_1.2_spmd.sunk | while | flops 1207959552 | bytes 15728909 | solution.py:113
  32.1 5.0 convolution_bitcast_fusion.2
  41.9 5.0 convolution_bitcast_fusion.2
  51.9 5.0 convolution_bitcast_fusion.2
  61.7 5.0 convolution_bitcast_fusion.2
  70.3 8.1 %copy.28 = f32[2,4,8,96,384]{4,3,2,1,0:T(8,128)} copy(f32[2,4,8,96,384]{4,3,0,2,1:T(8,128)} %bitcast.70) | data formatting | bytes 18874368 | tf_op jit(solution)/shard_map/transpose | solution.py:40
  78.5 27.6 %reduce-scatter.4.cloned.1.call-done = f32[32,96,384]{2,1,0:T(8,128)} async-done(((f32[64,96,384]{2,1,0:T(8,128)}), f32[32,96,384]{2,1,0:T(8,128)}) %reduce-scatter.4.cloned.1.call-update) | async-done | bytes 4718608 | tf_op jit(solution)/shard_map/reduce_scatter | solution.py:43
  106.1 57.0 %reduce-scatter.6.cloned.1.call-done = f32[8,96,384]{2,1,0:T(8,128)} async-done(((f32[32,96,384]{2,1,0:T(8,128)}), f32[8,96,384]{2,1,0:T(8,128)}) %reduce-scatter.6.cloned.1.call-update) | async-done | bytes 1179664 | tf_op jit(solution)/shard_map/reduce_scatter | solution.py:43
  163.2 36.9 %reduce-scatter.8.cloned.1.call-done = f32[1,96,384]{2,1,0:T(8,128)} async-done(((f32[8,96,384]{2,1,0:T(8,128)}), f32[1,96,384]{2,1,0:T(8,128)}) %reduce-scatter.8.cloned.1.call-update) | async-done | bytes 147472 | tf_op jit(solution)/shard_map/reduce_scatter | solution.py:43
  201.0 8.1 %all_to_all.45 = bf16[4,24,384]{2,1,0:T(8,128)(2,1)S(1)} all-to-all(bf16[4,24,384]{2,1,0:T(8,128)(2,1)S(1)} %bitcast.80), channel_id=1, replica_groups=mesh['replica_0'=4,'replica_1'=8,'replica_2'=2,'shard'=4] {'shard'}, dimensions={0} | all-to-all | bytes 147456 | tf_op jit(solution)/shard_map/all_to_all | solution.py:119
  209.2 8.1 %all_to_all.46 = bf16[4,24,1536]{2,1,0:T(8,128)(2,1)S(1)} all-to-all(bf16[4,24,1536]{2,1,0:T(8,128)(2,1)S(1)} %broadcast_in_dim.44), channel_id=1, replica_groups=mesh['replica_0'=4,'replica_1'=8,'replica_2'=2,'shard'=4] {'shard'}, dimensions={0} | all-to-all | bytes 589824 | tf_op jit(solution)/shard_map/all_to_all | solution.py:26
  217.2 7.8 %collective-permute-start = (bf16[96,1536]{1,0:T(8,128)(2,1)S(1)}, bf16[96,1536]{1,0:T(8,128)(2,1)S(1)}, u32[]{:S(2)}, u32[]{:S(2)}) collective-permute-start(bf16[96,1536]{1,0:T(8,128)(2,1)S(1)} %bitcast.72), channel_id=1, source_target_pairs={{0,4},{4,0},{8,12},{12,8},{16,20},{20,16},{24,28},{28,24},{32,36},... | collective-permute-start | bytes 884744 | tf_op jit(solution)/shard_map/ppermute | solution.py:34
  228.1 3.5 all-to-all-start.2
  231.6 6.1 all-to-all-done.2
  244.8 35.8 %collective-permute-done.5 = bf16[192,1536]{1,0:T(8,128)(2,1)S(1)} collective-permute-done((bf16[192,1536]{1,0:T(8,128)(2,1)S(1)}, bf16[192,1536]{1,0:T(8,128)(2,1)S(1)}, u32[]{:S(2)}, u32[]{:S(2)}) %collective-permute-start.5) | collective-permute-done | bytes 589856 | tf_op jit(solution)/shard_map/ppermute | solution.py:34
  282.9 37.5 %collective-permute-done.2 = bf16[384,1536]{1,0:T(8,128)(2,1)} collective-permute-done((bf16[384,1536]{1,0:T(8,128)(2,1)S(1)}, bf16[384,1536]{1,0:T(8,128)(2,1)}, u32[]{:S(2)}, u32[]{:S(2)}) %collective-permute-start.2) | collective-permute-done | bytes 1179680 | tf_op jit(solution)/shard_map/ppermute | solution.py:34
  320.4 2.7 maximum_select_fusion.3
  325.6 71.3 %collective-permute-done.6 = bf16[384,1536]{1,0:T(8,128)(2,1)S(1)} collective-permute-done((bf16[384,1536]{1,0:T(8,128)(2,1)S(1)}, bf16[384,1536]{1,0:T(8,128)(2,1)S(1)}, u32[]{:S(2)}, u32[]{:S(2)}) %collective-permute-start.6) | collective-permute-done | bytes 1179680 | tf_op jit(solution)/shard_map/ppermute | solution.py:34
  403.8 4.0 maximum_select_fusion
  410.7 142.4 %collective-permute-done.7 = bf16[768,1536]{1,0:T(8,128)(2,1)} collective-permute-done((bf16[768,1536]{1,0:T(8,128)(2,1)}, bf16[768,1536]{1,0:T(8,128)(2,1)}, u32[]{:S(2)}, u32[]{:S(2)}) %collective-permute-start.7) | collective-permute-done | bytes 2359328 | tf_op jit(solution)/shard_map/ppermute | solution.py:34
  553.1 7.1 %multiply_reduce_fusion = (f32[]{:T(128)}, f32[24,1536]{1,0:T(8,128)S(1)}) fusion(f32[1536,24]{0,1:T(8,128)S(1)} %fusion.19, bf16[768,1536]{1,0:T(8,128)(2,1)} %maximum_select_fusion.4, bf16[768,1536]{1,0:T(8,128)(2,1)} %collective-permute-done.7, pred[]{:T(512)S(6)} %eq.40), kind=kOutput, calls=%fused_computation.41 | convolution fusion | flops 700784640 | bytes 5013509 | tf_op jit(solution)/shard_map/dot_general | solution.py:144
  560.8 8.3 %all-reduce.2 = (f32[4]{0:T(128)S(1)}, f32[4]{0:T(128)S(1)}) all-reduce(f32[4]{0:T(128)S(1)} %fusion.22, f32[4]{0:T(128)S(1)} %fusion.21), channel_id=1, replica_groups=mesh['replica_0'=4,'replica_1'=8,'replica_2'=2,'shard'=4] {'replica_0'}, use_global_device_ids=true, to_apply=%region_7.8 | all-reduce | flops 8 | bytes 64 | tf_op jit(solution)/shard_map/psum | solution.py:58
  569.1 11.1 %all-reduce = (f32[4]{0:T(128)S(1)}, f32[4]{0:T(128)S(1)}) all-reduce(f32[4]{0:T(128)S(1)} %get-tuple-element.107, f32[4]{0:T(128)S(1)} %get-tuple-element.108), channel_id=1, replica_groups=mesh['replica_0'=4,'replica_1'=8,'replica_2'=2,'shard'=4] {'replica_1'}, use_global_device_ids=true, to_apply=%region_8.9 | all-reduce | flops 8 | bytes 64 | tf_op jit(solution)/shard_map/psum | solution.py:58
  580.2 8.4 %all-reduce.3 = (f32[4]{0:T(128)S(1)}, f32[4]{0:T(128)S(1)}) all-reduce(f32[4]{0:T(128)S(1)} %get-tuple-element.103, f32[4]{0:T(128)S(1)} %get-tuple-element.104), channel_id=1, replica_groups=mesh['replica_0'=4,'replica_1'=8,'replica_2'=2,'shard'=4] {'replica_2'}, use_global_device_ids=true, to_apply=%region_9.10 | all-reduce | flops 8 | bytes 64 | tf_op jit(solution)/shard_map/psum | solution.py:58
  588.6 6.8 all-reduce.1
  597.6 7.6 %all_to_all.47 = bf16[24,4,384]{2,0,1:T(8,128)(2,1)} all-to-all(bf16[24,4,384]{2,0,1:T(8,128)(2,1)S(1)} %bitcast.84), channel_id=1, replica_groups=mesh['replica_0'=4,'replica_1'=8,'replica_2'=2,'shard'=4] {'shard'}, dimensions={1} | all-to-all | bytes 147456 | tf_op jit(solution)/shard_map/all_to_all | solution.py:159
  605.5 3.6 fusion.12
  611.5 70.9 %all-gather.2.cloned.1.call-done = bf16[6144,384]{1,0:T(8,128)(2,1)} async-done(((bf16[96,384]{1,0:T(8,128)(2,1)}), bf16[6144,384]{1,0:T(8,128)(2,1)}) %all-gather.2.cloned.1.call-update) | async-done | bytes 4718608 | tf_op jit(solution)/shard_map/all_gather | solution.py:160
  682.4 5.9 gather_fusion.1
  688.3 5.1 broadcast_select_fusion
  (83 shorter events, 49.9 us)
Async XLA Ops:
  7.2 1.9 copy-start
  7.2 98.9 %reduce-scatter.4.cloned.1.call-start = ((), (), s32[]{:S(2)}) async-start(), calls=%async_computation.7 | async-start | bytes 14155776 | tf_op jit(solution)/shard_map/reduce_scatter | solution.py:43
  78.4 84.7 %reduce-scatter.6.cloned.1.call-start = ((), (), s32[]{:S(2)}) async-start(), calls=%async_computation.8 | async-start | bytes 5898240 | tf_op jit(solution)/shard_map/reduce_scatter | solution.py:43
  106.0 121.1 %copy-start.5 = (bf16[24,2,1536]{2,1,0:T(2,128)(2,1)S(1)}, bf16[24,2,1536]{2,1,0:T(2,128)(2,1)}, u32[]{:S(2)}) copy-start(bf16[24,2,1536]{2,1,0:T(2,128)(2,1)} %param.15) | copy-start | bytes 442372
  106.1 94.0 %reduce-scatter.8.cloned.1.call-start = ((), (), s32[]{:S(2)}) async-start(), calls=%async_computation.9 | async-start | bytes 1327104 | tf_op jit(solution)/shard_map/reduce_scatter | solution.py:43
  217.2 9.0 %collective-permute-start = (bf16[96,1536]{1,0:T(8,128)(2,1)S(1)}, bf16[96,1536]{1,0:T(8,128)(2,1)S(1)}, u32[]{:S(2)}, u32[]{:S(2)}) collective-permute-start(bf16[96,1536]{1,0:T(8,128)(2,1)S(1)} %bitcast.72), channel_id=1, source_target_pairs={{0,4},{4,0},{8,12},{12,8},{16,20},{20,16},{24,28},{28,24},{32,36},... | collective-permute-start | bytes 884744 | tf_op jit(solution)/shard_map/ppermute | solution.py:34
  226.3 14.6 %collective-permute-start.1 = (bf16[192,1536]{1,0:T(8,128)(2,1)S(1)}, bf16[192,1536]{1,0:T(8,128)(2,1)S(1)}, u32[]{:S(2)}, u32[]{:S(2)}) collective-permute-start(bf16[192,1536]{1,0:T(8,128)(2,1)S(1)} %maximum_select_fusion.7), channel_id=1, source_target_pairs={{0,8},{4,12},{8,0},{12,4},{16,24},{20,28},{24,16},{28,20},{32,40},... | collective-permute-start | bytes 1769480 | tf_op jit(solution)/shard_map/ppermute | solution.py:34
  228.1 9.6 %all-to-all-start.2 = ((bf16[4,24,1536]{2,1,0:T(8,128)(2,1)}), bf16[4,24,1536]{2,1,0:T(8,128)(2,1)S(1)}, u32[]{:S(2)}, u32[]{:S(2)}) async-start(bf16[4,24,1536]{2,1,0:T(8,128)(2,1)} %broadcast_in_dim.46), calls=%async_computation.5 | async-start | bytes 589824 | tf_op jit(solution)/shard_map/all_to_all | solution.py:26
  231.5 450.9 %all-gather.2.cloned.1.call-start = ((), (), s32[]{:S(2)}) async-start(), calls=%async_computation.10 | async-start | bytes 4792320 | tf_op jit(solution)/shard_map/all_gather | solution.py:160
  237.7 5.8 collective-permute-start.4
  241.4 41.5 %copy-start.4 = (bf16[384,1536]{1,0:T(8,128)(2,1)}, bf16[384,1536]{1,0:T(8,128)(2,1)S(1)}, u32[]{:S(2)}) copy-start(bf16[384,1536]{1,0:T(8,128)(2,1)S(1)} %maximum_select_fusion.5) | copy-start | bytes 3538948
  241.4 79.0 %collective-permute-start.2 = (bf16[384,1536]{1,0:T(8,128)(2,1)S(1)}, bf16[384,1536]{1,0:T(8,128)(2,1)}, u32[]{:S(2)}, u32[]{:S(2)}) collective-permute-start(bf16[384,1536]{1,0:T(8,128)(2,1)S(1)} %maximum_select_fusion.5), channel_id=1, source_target_pairs={{0,16},{4,20},{8,24},{12,28},{16,0},{20,4},{24,8},{28,12},{32,48},... | collective-permute-start | bytes 3538952 | tf_op jit(solution)/shard_map/ppermute | solution.py:34
  243.6 37.0 %collective-permute-start.5 = (bf16[192,1536]{1,0:T(8,128)(2,1)S(1)}, bf16[192,1536]{1,0:T(8,128)(2,1)S(1)}, u32[]{:S(2)}, u32[]{:S(2)}) collective-permute-start(bf16[192,1536]{1,0:T(8,128)(2,1)S(1)} %maximum_select_fusion.8), channel_id=1, source_target_pairs={{0,8},{4,12},{8,0},{12,4},{16,24},{20,28},{24,16},{28,20},{32,40},... | collective-permute-start | bytes 1769480 | tf_op jit(solution)/shard_map/ppermute | solution.py:34
  280.9 115.9 %collective-permute-start.6 = (bf16[384,1536]{1,0:T(8,128)(2,1)S(1)}, bf16[384,1536]{1,0:T(8,128)(2,1)S(1)}, u32[]{:S(2)}, u32[]{:S(2)}) collective-permute-start(bf16[384,1536]{1,0:T(8,128)(2,1)S(1)} %maximum_select_fusion.6), channel_id=1, source_target_pairs={{0,16},{4,20},{8,24},{12,28},{16,0},{20,4},{24,8},{28,12},{32,48},... | collective-permute-start | bytes 3538952 | tf_op jit(solution)/shard_map/ppermute | solution.py:34
  323.1 78.6 %copy-start.7 = (f32[24,1536]{1,0:T(8,128)S(1)}, f32[24,1536]{1,0:T(8,128)}, u32[]{:S(2)}) copy-start(f32[24,1536]{1,0:T(8,128)} %param.17) | copy-start | bytes 442372
  323.1 78.6 %copy-start.8 = (f32[24,1536]{1,0:T(8,128)S(1)}, f32[24,1536]{1,0:T(8,128)}, u32[]{:S(2)}) copy-start(f32[24,1536]{1,0:T(8,128)} %param.16) | copy-start | bytes 442372
  323.1 80.8 %collective-permute-start.3 = (bf16[768,1536]{1,0:T(8,128)(2,1)S(1)}, bf16[768,1536]{1,0:T(8,128)(2,1)}, u32[]{:S(2)}, u32[]{:S(2)}) collective-permute-start(bf16[768,1536]{1,0:T(8,128)(2,1)S(1)} %maximum_select_fusion.3), channel_id=1, source_target_pairs={{0,32},{4,36},{8,40},{12,44},{16,48},{20,52},{24,56},{28,60},{32,0... | collective-permute-start | bytes 7077896 | tf_op jit(solution)/shard_map/ppermute | solution.py:34
  398.6 154.5 %collective-permute-start.7 = (bf16[768,1536]{1,0:T(8,128)(2,1)}, bf16[768,1536]{1,0:T(8,128)(2,1)}, u32[]{:S(2)}, u32[]{:S(2)}) collective-permute-start(bf16[768,1536]{1,0:T(8,128)(2,1)} %maximum_select_fusion.4), channel_id=1, source_target_pairs={{0,32},{4,36},{8,40},{12,44},{16,48},{20,52},{24,56},{28,60},{32,0... | collective-permute-start | bytes 7077896 | tf_op jit(solution)/shard_map/ppermute | solution.py:34
  407.8 2.2 copy-start.2
  410.7 194.5 %copy-start.9 = (s32[4]{0:T(128)S(1)}, s32[4]{0:T(128)}, u32[]{:S(2)}) copy-start(s32[4]{0:T(128)} %param.12) | copy-start | bytes 52
  410.7 194.5 %copy-start.6 = (f32[24,2,1536]{2,1,0:T(2,128)S(1)}, f32[24,2,1536]{2,1,0:T(2,128)}, u32[]{:S(2)}) copy-start(f32[24,2,1536]{2,1,0:T(2,128)} %param.14) | copy-start | bytes 884740
  605.2 4.0 copy-start.3
  682.4 11.0 %copy-start.1 = (bf16[1024,4,384]{2,1,0:T(4,128)(2,1)S(1)}, bf16[1024,4,384]{2,1,0:T(4,128)(2,1)}, u32[]{:S(2)}) copy-start(bf16[1024,4,384]{2,1,0:T(4,128)(2,1)} %param.11) | copy-start | bytes 9437188
Sparse Core Ops, SparseCore 0:
  78.5 27.4 reduce-scatter.3
  108.6 54.5 reduce-scatter.5
  165.7 34.3 reduce-scatter.7
  605.3 77.0 all-gather.1
where the time goes:
time: 701 us; the launch traced here: 700 us
  waiting for transfers between devices  488 us (70%)
  blocking collectives  58.3 us (8%)
  local copies, waits for them, and re-layouts  54.7 us (8%)
  matrix products  32.5 us (5%)
  starting transfers between devices  24 us (3%)
  other arithmetic  23.2 us (3%)
  between operations  16.3 us (2%)
    ppermute x8, waiting for transfers between devices, partner_2(): lax.ppermute(value, axis, [(i, i ^ 1 << apart) for i in range(lax.axis_si...  290 us
    reduce_scatter x3, waiting for transfers between devices, reduced_to_own(): pieces = lax.psum_scatter(pieces, axes[k], scatter_dimension=0, tiled=True)  122 us
    all_gather x1, waiting for transfers between devices, body(): every_block = lax.all_gather(feature_rows, REPLICA, axis=0, tiled=True)  70.9 us
    psum x4, blocking collectives, one_axis_at_a_time(): return functools.reduce(lax.psum, axes, value)  34.6 us
    ppermute x8, starting transfers between devices, partner_2(): lax.ppermute(value, axis, [(i, i ^ 1 << apart) for i in range(lax.axis_si...  20.4 us
    dot_general x4, matrix products, piece_product(): lax.dot_general(activations, douts, (((0,), (0,)), ((), ())), preferred_e...  19.8 us
    gather x1, local copies, waits for them, and re-layouts, body(): grads_slot = jnp.take(output_grads, source, axis=1)  16.4 us
    dynamic_update_slice x8, local copies, waits for them, and re-layouts, body(): lax.map(piece_product, jnp.arange(rows_dev * lax.axis_size(REPLICA) // pi...  14.5 us
  transfers between devices with their start and end apart: 13, of which 11 were waited for; matrix products, arithmetic and copies ran while one was open for 3% of the time, Pallas kernels for 0%

commit v1 on v0

--- a/solution.py
+++ b/solution.py
@@ -157,7 +157,12 @@
     scale = jnp.sqrt(adam_squares) / (jnp.sqrt(precond_squares) + eps_norm)
     grafted = (precond * scale).astype(jnp.bfloat16)
     feature_rows = lax.all_to_all(grafted, "shard", split_axis=1, concat_axis=0, tiled=True)
-    every_block = lax.all_gather(feature_rows, REPLICA, axis=0, tiled=True)
+    every_block = jnp.concatenate(
+        lax.all_to_all(
+            jnp.stack([feature_rows for _ in range(lax.axis_size(REPLICA))], 0), REPLICA, 0, 0
+        ),
+        axis=0,
+    )
     update = jnp.take(
         every_block.reshape(blocks_count, model_width, every_block.shape[-1]), owner, axis=0
     )

time: 701 us -> 742 us (1.058)
  waiting for transfers between devices: 488 us -> 517 us
  starting transfers between devices: 24 us -> 32.3 us
    all_to_all x0 -> x1, waiting for transfers between devices: none -> 98.8 us  [body(): lax.all_to_all(jnp.stack([feature_rows for _ in range(lax.axis_size(REPLI...]
    all_gather x1 -> x0, waiting for transfers between devices: 70.9 us -> none  [body(): every_block = lax.all_gather(feature_rows, REPLICA, axis=0, tiled=True)]
    all_to_all x0 -> x1, starting transfers between devices: none -> 8.74 us  [body(): lax.all_to_all(jnp.stack([feature_rows for _ in range(lax.axis_size(REPLI...]
where the time goes in v1:
time: 742 us; the launch traced here: 741 us
  waiting for transfers between devices  517 us (70%)
  blocking collectives  57.8 us (8%)
  local copies, waits for them, and re-layouts  57.1 us (8%)
  matrix products  34.9 us (5%)
  starting transfers between devices  32.3 us (4%)
  other arithmetic  22.9 us (3%)
  between operations  16.2 us (2%)
    ppermute x8, waiting for transfers between devices, partner_2(): lax.ppermute(value, axis, [(i, i ^ 1 << apart) for i in range(lax.axis_si...  290 us
    reduce_scatter x3, waiting for transfers between devices, reduced_to_own(): pieces = lax.psum_scatter(pieces, axes[k], scatter_dimension=0, tiled=True)  122 us
    all_to_all x1, waiting for transfers between devices, body(): lax.all_to_all(jnp.stack([feature_rows for _ in range(lax.axis_size(REPLI...  98.8 us
    psum x4, blocking collectives, one_axis_at_a_time(): return functools.reduce(lax.psum, axes, value)  34.6 us
    ppermute x8, starting transfers between devices, partner_2(): lax.ppermute(value, axis, [(i, i ^ 1 << apart) for i in range(lax.axis_si...  20 us
    dot_general x4, matrix products, piece_product(): lax.dot_general(activations, douts, (((0,), (0,)), ((), ())), preferred_e...  19.9 us
    gather x1, local copies, waits for them, and re-layouts, body(): grads_slot = jnp.take(output_grads, source, axis=1)  16.4 us
  transfers between devices with their start and end apart: 13, of which 11 were waited for; matrix products, arithmetic and copies ran while one was open for 3% of the time, Pallas kernels for 0%

profile of v1, /device:TPU:1, one launch (start us, length us, event | category | flops | bytes accessed | tf_op | source)
XLA Modules:
  0.0 740.6 jit_solution(17878925359848535890)
XLA Ops:
  9.1 16.4 %gather_fusion = bf16[4,1024,384]{2,0,1:T(4,128)(2,1)} fusion(bf16[1024,4,384]{2,1,0:T(4,128)(2,1)S(1)} %copy-done, s32[1024]{0:T(1024)S(1)} %pad_clamp_fusion.1), kind=kCustom, calls=%fused_computation | custom fusion | bytes 6291472 | tf_op jit(solution)/shard_map/jit(_take)/gather | solution.py:102
  30.9 39.4 %while.12 = (s32[]{:T(128)}, f32[4,1536,384]{2,1,0:T(8,128)}, s32[4]{0:T(128)S(1)}, bf16[1024,4,384]{2,0,1:T(8,128)(2,1)}, bf16[1024,1536]{1,0:T(8,128)(2,1)}, /...) while((s32[]{:T(128)}, f32[4,1536,384]{2,1,0:T(8,128)}, ...), condition=%wide.region_2.3_spmd, body=%wide.region_1.2_spmd.sunk | while | flops 1207959552 | bytes 15728909 | solution.py:113
  32.1 5.0 convolution_bitcast_fusion.2
  42.0 5.0 convolution_bitcast_fusion.2
  51.9 5.0 convolution_bitcast_fusion.2
  61.7 5.0 convolution_bitcast_fusion.2
  70.3 8.1 %copy.28 = f32[2,4,8,96,384]{4,3,2,1,0:T(8,128)} copy(f32[2,4,8,96,384]{4,3,0,2,1:T(8,128)} %bitcast.70) | data formatting | bytes 18874368 | tf_op jit(solution)/shard_map/transpose | solution.py:40
  78.5 27.6 %reduce-scatter.4.cloned.1.call-done = f32[32,96,384]{2,1,0:T(8,128)} async-done(((f32[64,96,384]{2,1,0:T(8,128)}), f32[32,96,384]{2,1,0:T(8,128)}) %reduce-scatter.4.cloned.1.call-update) | async-done | bytes 4718608 | tf_op jit(solution)/shard_map/reduce_scatter | solution.py:43
  106.2 57.0 %reduce-scatter.6.cloned.1.call-done = f32[8,96,384]{2,1,0:T(8,128)} async-done(((f32[32,96,384]{2,1,0:T(8,128)}), f32[8,96,384]{2,1,0:T(8,128)}) %reduce-scatter.6.cloned.1.call-update) | async-done | bytes 1179664 | tf_op jit(solution)/shard_map/reduce_scatter | solution.py:43
  163.2 37.1 %reduce-scatter.8.cloned.1.call-done = f32[1,96,384]{2,1,0:T(8,128)} async-done(((f32[8,96,384]{2,1,0:T(8,128)}), f32[1,96,384]{2,1,0:T(8,128)}) %reduce-scatter.8.cloned.1.call-update) | async-done | bytes 147472 | tf_op jit(solution)/shard_map/reduce_scatter | solution.py:43
  201.2 8.2 %all_to_all.47 = bf16[4,24,384]{2,1,0:T(8,128)(2,1)S(1)} all-to-all(bf16[4,24,384]{2,1,0:T(8,128)(2,1)S(1)} %bitcast.79), channel_id=1, replica_groups=mesh['replica_0'=4,'replica_1'=8,'replica_2'=2,'shard'=4] {'shard'}, dimensions={0} | all-to-all | bytes 147456 | tf_op jit(solution)/shard_map/all_to_all | solution.py:119
  209.5 8.1 %all_to_all.48 = bf16[4,24,1536]{2,1,0:T(8,128)(2,1)S(1)} all-to-all(bf16[4,24,1536]{2,1,0:T(8,128)(2,1)S(1)} %broadcast_in_dim.44), channel_id=1, replica_groups=mesh['replica_0'=4,'replica_1'=8,'replica_2'=2,'shard'=4] {'shard'}, dimensions={0} | all-to-all | bytes 589824 | tf_op jit(solution)/shard_map/all_to_all | solution.py:26
  217.5 7.5 %collective-permute-start = (bf16[96,1536]{1,0:T(8,128)(2,1)S(1)}, bf16[96,1536]{1,0:T(8,128)(2,1)S(1)}, u32[]{:S(2)}, u32[]{:S(2)}) collective-permute-start(bf16[96,1536]{1,0:T(8,128)(2,1)S(1)} %bitcast.71), channel_id=1, source_target_pairs={{0,4},{4,0},{8,12},{12,8},{16,20},{20,16},{24,28},{28,24},{32,36},... | collective-permute-start | bytes 884744 | tf_op jit(solution)/shard_map/ppermute | solution.py:34
  228.1 3.5 all-to-all-start.2
  231.6 6.1 all-to-all-done.2
  244.8 35.8 %collective-permute-done.5 = bf16[192,1536]{1,0:T(8,128)(2,1)S(1)} collective-permute-done((bf16[192,1536]{1,0:T(8,128)(2,1)S(1)}, bf16[192,1536]{1,0:T(8,128)(2,1)S(1)}, u32[]{:S(2)}, u32[]{:S(2)}) %collective-permute-start.5) | collective-permute-done | bytes 589856 | tf_op jit(solution)/shard_map/ppermute | solution.py:34
  282.8 37.6 %collective-permute-done.2 = bf16[384,1536]{1,0:T(8,128)(2,1)} collective-permute-done((bf16[384,1536]{1,0:T(8,128)(2,1)S(1)}, bf16[384,1536]{1,0:T(8,128)(2,1)}, u32[]{:S(2)}, u32[]{:S(2)}) %collective-permute-start.2) | collective-permute-done | bytes 1179680 | tf_op jit(solution)/shard_map/ppermute | solution.py:34
  325.6 71.3 %collective-permute-done.6 = bf16[384,1536]{1,0:T(8,128)(2,1)S(1)} collective-permute-done((bf16[384,1536]{1,0:T(8,128)(2,1)S(1)}, bf16[384,1536]{1,0:T(8,128)(2,1)S(1)}, u32[]{:S(2)}, u32[]{:S(2)}) %collective-permute-start.6) | collective-permute-done | bytes 1179680 | tf_op jit(solution)/shard_map/ppermute | solution.py:34
  403.9 3.8 maximum_select_fusion
  410.6 142.5 %collective-permute-done.7 = bf16[768,1536]{1,0:T(8,128)(2,1)} collective-permute-done((bf16[768,1536]{1,0:T(8,128)(2,1)}, bf16[768,1536]{1,0:T(8,128)(2,1)}, u32[]{:S(2)}, u32[]{:S(2)}) %collective-permute-start.7) | collective-permute-done | bytes 2359328 | tf_op jit(solution)/shard_map/ppermute | solution.py:34
  553.1 7.2 multiply_reduce_fusion
  561.0 8.4 %all-reduce.2 = (f32[4]{0:T(128)S(1)}, f32[4]{0:T(128)S(1)}) all-reduce(f32[4]{0:T(128)S(1)} %fusion.22, f32[4]{0:T(128)S(1)} %fusion.21), channel_id=1, replica_groups=mesh['replica_0'=4,'replica_1'=8,'replica_2'=2,'shard'=4] {'replica_0'}, use_global_device_ids=true, to_apply=%region_7.8 | all-reduce | flops 8 | bytes 64 | tf_op jit(solution)/shard_map/psum | solution.py:58
  569.4 11.0 %all-reduce = (f32[4]{0:T(128)S(1)}, f32[4]{0:T(128)S(1)}) all-reduce(f32[4]{0:T(128)S(1)} %get-tuple-element.107, f32[4]{0:T(128)S(1)} %get-tuple-element.108), channel_id=1, replica_groups=mesh['replica_0'=4,'replica_1'=8,'replica_2'=2,'shard'=4] {'replica_1'}, use_global_device_ids=true, to_apply=%region_8.9 | all-reduce | flops 8 | bytes 64 | tf_op jit(solution)/shard_map/psum | solution.py:58
  580.4 8.4 %all-reduce.3 = (f32[4]{0:T(128)S(1)}, f32[4]{0:T(128)S(1)}) all-reduce(f32[4]{0:T(128)S(1)} %get-tuple-element.103, f32[4]{0:T(128)S(1)} %get-tuple-element.104), channel_id=1, replica_groups=mesh['replica_0'=4,'replica_1'=8,'replica_2'=2,'shard'=4] {'replica_2'}, use_global_device_ids=true, to_apply=%region_9.10 | all-reduce | flops 8 | bytes 64 | tf_op jit(solution)/shard_map/psum | solution.py:58
  588.8 6.8 all-reduce.1
  597.7 6.9 all_to_all.49
  607.1 8.7 %all-to-all-start.4 = ((bf16[64,96,384]{2,1,0:T(8,128)(2,1)}), bf16[64,96,384]{2,1,0:T(8,128)(2,1)}, u32[]{:S(2)}, u32[]{:S(2)}) async-start(bf16[64,96,384]{2,1,0:T(8,128)(2,1)} %stack.14), calls=%async_computation.7 | async-start | bytes 9437184 | tf_op jit(solution)/shard_map/all_to_all | solution.py:161
  616.2 3.4 fusion.12
  619.6 3.7 fusion.13
  624.3 98.8 %all-to-all-done.4 = bf16[64,96,384]{2,1,0:T(8,128)(2,1)} async-done(((bf16[64,96,384]{2,1,0:T(8,128)(2,1)}), bf16[64,96,384]{2,1,0:T(8,128)(2,1)}, u32[]{:S(2)}, u32[]{:S(2)}) %all-to-all-start.4) | async-done | bytes 4718624 | tf_op jit(solution)/shard_map/all_to_all | solution.py:161
  723.1 5.9 gather_fusion.1
  728.9 5.1 broadcast_select_fusion
  (81 shorter events, 56.8 us)
Async XLA Ops:
  7.2 1.9 copy-start
  7.2 98.9 %reduce-scatter.4.cloned.1.call-start = ((), (), s32[]{:S(2)}) async-start(), calls=%async_computation.8 | async-start | bytes 14155776 | tf_op jit(solution)/shard_map/reduce_scatter | solution.py:43
  78.4 84.7 %reduce-scatter.6.cloned.1.call-start = ((), (), s32[]{:S(2)}) async-start(), calls=%async_computation.9 | async-start | bytes 5898240 | tf_op jit(solution)/shard_map/reduce_scatter | solution.py:43
  106.1 121.1 %copy-start.4 = (bf16[24,2,1536]{2,1,0:T(2,128)(2,1)S(1)}, bf16[24,2,1536]{2,1,0:T(2,128)(2,1)}, u32[]{:S(2)}) copy-start(bf16[24,2,1536]{2,1,0:T(2,128)(2,1)} %param.15) | copy-start | bytes 442372
  106.1 94.1 %reduce-scatter.8.cloned.1.call-start = ((), (), s32[]{:S(2)}) async-start(), calls=%async_computation.10 | async-start | bytes 1327104 | tf_op jit(solution)/shard_map/reduce_scatter | solution.py:43
  217.5 8.7 %collective-permute-start = (bf16[96,1536]{1,0:T(8,128)(2,1)S(1)}, bf16[96,1536]{1,0:T(8,128)(2,1)S(1)}, u32[]{:S(2)}, u32[]{:S(2)}) collective-permute-start(bf16[96,1536]{1,0:T(8,128)(2,1)S(1)} %bitcast.71), channel_id=1, source_target_pairs={{0,4},{4,0},{8,12},{12,8},{16,20},{20,16},{24,28},{28,24},{32,36},... | collective-permute-start | bytes 884744 | tf_op jit(solution)/shard_map/ppermute | solution.py:34
  226.4 14.6 %collective-permute-start.1 = (bf16[192,1536]{1,0:T(8,128)(2,1)S(1)}, bf16[192,1536]{1,0:T(8,128)(2,1)S(1)}, u32[]{:S(2)}, u32[]{:S(2)}) collective-permute-start(bf16[192,1536]{1,0:T(8,128)(2,1)S(1)} %maximum_select_fusion.7), channel_id=1, source_target_pairs={{0,8},{4,12},{8,0},{12,4},{16,24},{20,28},{24,16},{28,20},{32,40},... | collective-permute-start | bytes 1769480 | tf_op jit(solution)/shard_map/ppermute | solution.py:34
  228.1 9.6 %all-to-all-start.2 = ((bf16[4,24,1536]{2,1,0:T(8,128)(2,1)}), bf16[4,24,1536]{2,1,0:T(8,128)(2,1)S(1)}, u32[]{:S(2)}, u32[]{:S(2)}) async-start(bf16[4,24,1536]{2,1,0:T(8,128)(2,1)} %broadcast_in_dim.46), calls=%async_computation.5 | async-start | bytes 589824 | tf_op jit(solution)/shard_map/all_to_all | solution.py:26
  237.7 5.7 collective-permute-start.4
  241.4 41.4 %copy-start.3 = (bf16[384,1536]{1,0:T(8,128)(2,1)}, bf16[384,1536]{1,0:T(8,128)(2,1)S(1)}, u32[]{:S(2)}) copy-start(bf16[384,1536]{1,0:T(8,128)(2,1)S(1)} %maximum_select_fusion.5) | copy-start | bytes 3538948
  241.4 79.0 %collective-permute-start.2 = (bf16[384,1536]{1,0:T(8,128)(2,1)S(1)}, bf16[384,1536]{1,0:T(8,128)(2,1)}, u32[]{:S(2)}, u32[]{:S(2)}) collective-permute-start(bf16[384,1536]{1,0:T(8,128)(2,1)S(1)} %maximum_select_fusion.5), channel_id=1, source_target_pairs={{0,16},{4,20},{8,24},{12,28},{16,0},{20,4},{24,8},{28,12},{32,48},... | collective-permute-start | bytes 3538952 | tf_op jit(solution)/shard_map/ppermute | solution.py:34
  243.6 37.0 %collective-permute-start.5 = (bf16[192,1536]{1,0:T(8,128)(2,1)S(1)}, bf16[192,1536]{1,0:T(8,128)(2,1)S(1)}, u32[]{:S(2)}, u32[]{:S(2)}) collective-permute-start(bf16[192,1536]{1,0:T(8,128)(2,1)S(1)} %maximum_select_fusion.8), channel_id=1, source_target_pairs={{0,8},{4,12},{8,0},{12,4},{16,24},{20,28},{24,16},{28,20},{32,40},... | collective-permute-start | bytes 1769480 | tf_op jit(solution)/shard_map/ppermute | solution.py:34
  281.0 115.9 %collective-permute-start.6 = (bf16[384,1536]{1,0:T(8,128)(2,1)S(1)}, bf16[384,1536]{1,0:T(8,128)(2,1)S(1)}, u32[]{:S(2)}, u32[]{:S(2)}) collective-permute-start(bf16[384,1536]{1,0:T(8,128)(2,1)S(1)} %maximum_select_fusion.6), channel_id=1, source_target_pairs={{0,16},{4,20},{8,24},{12,28},{16,0},{20,4},{24,8},{28,12},{32,48},... | collective-permute-start | bytes 3538952 | tf_op jit(solution)/shard_map/ppermute | solution.py:34
  323.1 78.6 %copy-start.6 = (f32[24,1536]{1,0:T(8,128)S(1)}, f32[24,1536]{1,0:T(8,128)}, u32[]{:S(2)}) copy-start(f32[24,1536]{1,0:T(8,128)} %param.17) | copy-start | bytes 442372
  323.1 78.6 %copy-start.7 = (f32[24,1536]{1,0:T(8,128)S(1)}, f32[24,1536]{1,0:T(8,128)}, u32[]{:S(2)}) copy-start(f32[24,1536]{1,0:T(8,128)} %param.16) | copy-start | bytes 442372
  323.2 80.8 %collective-permute-start.3 = (bf16[768,1536]{1,0:T(8,128)(2,1)S(1)}, bf16[768,1536]{1,0:T(8,128)(2,1)}, u32[]{:S(2)}, u32[]{:S(2)}) collective-permute-start(bf16[768,1536]{1,0:T(8,128)(2,1)S(1)} %maximum_select_fusion.3), channel_id=1, source_target_pairs={{0,32},{4,36},{8,40},{12,44},{16,48},{20,52},{24,56},{28,60},{32,0... | collective-permute-start | bytes 7077896 | tf_op jit(solution)/shard_map/ppermute | solution.py:34
  398.7 154.4 %collective-permute-start.7 = (bf16[768,1536]{1,0:T(8,128)(2,1)}, bf16[768,1536]{1,0:T(8,128)(2,1)}, u32[]{:S(2)}, u32[]{:S(2)}) collective-permute-start(bf16[768,1536]{1,0:T(8,128)(2,1)} %maximum_select_fusion.4), channel_id=1, source_target_pairs={{0,32},{4,36},{8,40},{12,44},{16,48},{20,52},{24,56},{28,60},{32,0... | collective-permute-start | bytes 7077896 | tf_op jit(solution)/shard_map/ppermute | solution.py:34
  407.7 2.2 copy-start.2
  607.1 8.8 %copy-start.8 = (s32[4]{0:T(128)S(1)}, s32[4]{0:T(128)}, u32[]{:S(2)}) copy-start(s32[4]{0:T(128)} %param.12) | copy-start | bytes 52
  607.1 8.8 %copy-start.5 = (f32[24,2,1536]{2,1,0:T(2,128)S(1)}, f32[24,2,1536]{2,1,0:T(2,128)}, u32[]{:S(2)}) copy-start(f32[24,2,1536]{2,1,0:T(2,128)} %param.14) | copy-start | bytes 884740
  607.1 115.9 %all-to-all-start.4 = ((bf16[64,96,384]{2,1,0:T(8,128)(2,1)}), bf16[64,96,384]{2,1,0:T(8,128)(2,1)}, u32[]{:S(2)}, u32[]{:S(2)}) async-start(bf16[64,96,384]{2,1,0:T(8,128)(2,1)} %stack.14), calls=%async_computation.7 | async-start | bytes 9437184 | tf_op jit(solution)/shard_map/all_to_all | solution.py:161
  723.1 11.0 %copy-start.1 = (bf16[1024,4,384]{2,1,0:T(4,128)(2,1)S(1)}, bf16[1024,4,384]{2,1,0:T(4,128)(2,1)}, u32[]{:S(2)}) copy-start(bf16[1024,4,384]{2,1,0:T(4,128)(2,1)} %param.11) | copy-start | bytes 9437188
Sparse Core Ops, SparseCore 0:
  78.6 27.4 reduce-scatter.3
  108.7 54.4 reduce-scatter.5
  165.7 34.4 reduce-scatter.7
